TPU v7x, 32 devices: a whole 2x2x4 slice. The times are simulated.
32 devices in a mesh: fsdp: 8 (over z, x), ctx: 2 (over core), tp: 2 (over y).
Axes of the slice: x: 2, y: 2, z: 4, core: 2. Of those that a mesh axis runs over, the one named last changes fastest.
Arguments:
- inputs: bfloat16 [8, 320, 1024], P('fsdp', 'ctx'), may hold values from -11 to 11, as said below
- lengths: int32 [8], P('fsdp'), may hold values from 224 to 320, as said below
- grad_out: bfloat16 [8, 320, 1024], P('fsdp', 'ctx'), may hold values from -6 to 6
- ln1_gain: bfloat16 [1024], P(('fsdp', 'ctx')), may hold values from 0.099609375 to 1.8984375
- ln1_shift: bfloat16 [1024], P(('fsdp', 'ctx')), may hold values from -3 to 3
- w_qkv: bfloat16 [1024, 3, 1024], P(('fsdp', 'ctx'), None, 'tp'), may hold values from -0.1875 to 0.1875
- b_qv: bfloat16 [1024, 2], P(('fsdp', 'ctx'), 'tp'), may hold values from -3 to 3
- w_proj: bfloat16 [1024, 1024], P(('fsdp', 'ctx'), 'tp'), may hold values from -0.5 to 0.5
- b_proj: bfloat16 [1024], P(('fsdp', 'ctx')), may hold values from -3 to 3
- ln2_gain: bfloat16 [1024], P(('fsdp', 'ctx')), may hold values from 0.099609375 to 1.8984375
- ln2_shift: bfloat16 [1024], P(('fsdp', 'ctx')), may hold values from -3 to 3
- w_up: bfloat16 [1024, 4096], P(('fsdp', 'ctx'), 'tp'), may hold values from -0.1875 to 0.1875
- b_up: bfloat16 [2048, 2], P(('fsdp', 'ctx'), 'tp'), may hold values from -3 to 3
- w_down: bfloat16 [1024, 4096], P(('fsdp', 'ctx'), 'tp'), may hold values from -0.09375 to 0.09375
- b_down: bfloat16 [1024], P(('fsdp', 'ctx')), may hold values from -3 to 3
Outputs:
- output: bfloat16 [8, 320, 1024], P('fsdp', 'ctx')
- grad_inputs: float32 [8, 320, 1024], P('fsdp', 'ctx')
- grad_ln1_gain: float32 [1024], P(('fsdp', 'ctx'))
- grad_ln1_shift: float32 [1024], P(('fsdp', 'ctx'))
- grad_w_qkv: float32 [1024, 3, 1024], P(('fsdp', 'ctx'), None, 'tp')
- grad_b_qv: float32 [1024, 2], P(('fsdp', 'ctx'), 'tp')
- grad_w_proj: float32 [1024, 1024], P(('fsdp', 'ctx'), 'tp')
- grad_b_proj: float32 [1024], P(('fsdp', 'ctx'))
- grad_ln2_gain: float32 [1024], P(('fsdp', 'ctx'))
- grad_ln2_shift: float32 [1024], P(('fsdp', 'ctx'))
- grad_w_up: float32 [1024, 4096], P(('fsdp', 'ctx'), 'tp')
- grad_b_up: float32 [2048, 2], P(('fsdp', 'ctx'), 'tp')
- grad_w_down: float32 [1024, 4096], P(('fsdp', 'ctx'), 'tp')
- grad_b_down: float32 [1024], P(('fsdp', 'ctx'))
- rms: float32 [5], replicated
Inputs may be any that keep to these rules, and one draw needn't show every extreme that they name: The lengths 320 and 224 both occur in every draw. `inputs`: rows at or past an image's length are never read.
All inputs are finite; a program needn't handle non-finite values.
Results may differ from a plain program's by a relative error of at most 0.014.
Values may be sent and summed in bfloat16 or wider, within the bound.
No kernel may reach another device: no remote copies, remote signals or barrier semaphores. Data moves between devices by JAX's collectives and lax.ppermute only.
A program may use at most 128 MiB of HBM per device.

v0:
```python
from functools import partial
import jax
import jax.numpy as jnp
from jax import lax
from jax.sharding import PartitionSpec as P

D = 1024
HD = 64
EPSILON = 1e-06
MASK_FILL = -1e30


def layer_norm(values_in, gain, shift):
    mean_val = jnp.mean(values_in, axis=-1, keepdims=True)
    centered = values_in - mean_val
    spread = jnp.mean(centered * centered, axis=-1, keepdims=True)
    return centered * lax.rsqrt(spread + EPSILON) * gain + shift


def contract(left, right, left_dim, right_dim):
    return lax.dot_general(
        left, right, (((left_dim,), (right_dim,)), ((), ())), preferred_element_type=jnp.float32
    )


def attn_scores(query_heads, key_all, key_valid):
    scores = jnp.einsum(
        "bqhd,bkhd->bhqk", query_heads, key_all, preferred_element_type=jnp.float32
    ) * HD ** (-0.5)
    return jnp.where(key_valid[:, None, None, :], scores, MASK_FILL)


def body(
    inputs,
    lengths,
    grad_out,
    ln1_gain,
    ln1_shift,
    w_qkv,
    b_qv,
    w_proj,
    b_proj,
    ln2_gain,
    ln2_shift,
    w_up,
    b_up,
    w_down,
    b_down,
):
    gathered = (
        lax.all_gather(ln1_gain, ("fsdp", "ctx"), axis=0, tiled=True),
        lax.all_gather(ln1_shift, ("fsdp", "ctx"), axis=0, tiled=True),
        lax.all_gather(w_qkv, ("fsdp", "ctx"), axis=0, tiled=True),
        lax.all_gather(b_qv, ("fsdp", "ctx"), axis=0, tiled=True),
        lax.all_gather(w_proj, ("fsdp", "ctx"), axis=0, tiled=True),
        lax.all_gather(b_proj, ("fsdp", "ctx"), axis=0, tiled=True),
        lax.all_gather(ln2_gain, ("fsdp", "ctx"), axis=0, tiled=True),
        lax.all_gather(ln2_shift, ("fsdp", "ctx"), axis=0, tiled=True),
        lax.all_gather(w_up, ("fsdp", "ctx"), axis=0, tiled=True),
        lax.all_gather(b_up, ("fsdp", "ctx"), axis=0, tiled=True),
        lax.all_gather(w_down, ("fsdp", "ctx"), axis=0, tiled=True),
        lax.all_gather(b_down, ("fsdp", "ctx"), axis=0, tiled=True),
    )
    (
        gain_first,
        shift_first,
        qkv_full,
        qv_bias,
        proj_full,
        proj_bias,
        gain_second,
        shift_second,
        up_full,
        up_bias,
        down_full,
        down_bias,
    ) = gathered
    images, half_slots = (inputs.shape[0], inputs.shape[1])
    row_count = images * half_slots
    slot_total = half_slots * lax.axis_size("ctx")
    slot_ids = lax.axis_index("ctx") * half_slots + jnp.arange(half_slots, dtype=jnp.int32)
    is_valid = (slot_ids[None, :] < lengths[:, None]).astype(jnp.float32)
    key_valid = jnp.arange(slot_total, dtype=jnp.int32)[None, :] < lengths[:, None]
    row_valid = is_valid.reshape(row_count, 1)
    gain_one = gain_first.astype(jnp.float32)
    shift_one = shift_first.astype(jnp.float32)
    gain_two = gain_second.astype(jnp.float32)
    shift_two = shift_second.astype(jnp.float32)
    entering = inputs.astype(jnp.float32).reshape(row_count, D) * row_valid
    normed = layer_norm(entering, gain_one, shift_one).astype(jnp.bfloat16)
    local_width = qkv_full.shape[2]
    local_heads = local_width // HD
    qkv_flat = qkv_full.reshape(D, 3 * local_width)
    packed = jnp.dot(normed, qkv_flat, preferred_element_type=jnp.float32).reshape(
        row_count, 3, local_width
    )
    bias_values = qv_bias.astype(jnp.float32)[:, 0]
    query_part = (packed[:, 0] + bias_values[:local_width]).astype(jnp.bfloat16)
    key_part = packed[:, 1].astype(jnp.bfloat16)
    value_part = (packed[:, 2] + bias_values[local_width:]).astype(jnp.bfloat16)
    head_shape = (images, half_slots, local_heads, HD)
    query_heads = query_part.reshape(head_shape)
    key_all, value_all = (
        lax.all_gather(key_part.reshape(head_shape), "ctx", axis=1, tiled=True),
        lax.all_gather(value_part.reshape(head_shape), "ctx", axis=1, tiled=True),
    )
    scores = attn_scores(query_heads, key_all, key_valid)
    row_max = jnp.max(scores, axis=-1, keepdims=True)
    raised = jnp.exp(scores - row_max)
    row_total = jnp.sum(raised, axis=-1, keepdims=True)
    attn_prob = raised / row_total
    log_total = row_max + jnp.log(row_total)
    context = jnp.einsum(
        "bhqk,bkhd->bqhd",
        attn_prob.astype(jnp.bfloat16),
        value_all,
        preferred_element_type=jnp.float32,
    )
    context = context.astype(jnp.bfloat16).reshape(row_count, local_width)
    attended = lax.psum(contract(context, proj_full, 1, 1), "tp") + proj_bias.astype(jnp.float32)
    middle = entering + attended
    normed_two = layer_norm(middle, gain_two, shift_two).astype(jnp.bfloat16)
    pre_act = (
        jnp.dot(normed_two, up_full, preferred_element_type=jnp.float32)
        + up_bias.astype(jnp.float32)[:, 0]
    )
    active = jax.nn.gelu(pre_act, approximate=False).astype(jnp.bfloat16)
    branch = lax.psum(contract(active, down_full, 1, 1).astype(jnp.bfloat16), "tp").astype(
        jnp.float32
    ) + down_bias.astype(jnp.float32)
    result = middle + branch
    output = result.astype(jnp.bfloat16).reshape(images, half_slots, D)
    square_sums = jnp.stack(
        [
            jnp.sum(row_valid * stat_term * stat_term)
            for stat_term in (entering, attended, middle, branch, result)
        ]
    )
    valid_count = jnp.sum(is_valid)
    total_squares, total_count = lax.psum((square_sums, valid_count), ("fsdp", "ctx"))
    rms = jnp.sqrt(total_squares / (total_count * D))
    grad_low = grad_out.reshape(row_count, D)
    grad_res = grad_low.astype(jnp.float32)
    grad_down_bias = jnp.sum(grad_res, axis=0)
    grad_down = contract(grad_low, active, 0, 0)
    grad_active = jnp.dot(grad_low, down_full, preferred_element_type=jnp.float32)
    _, gelu_pull = jax.vjp(partial(jax.nn.gelu, approximate=False), pre_act)
    grad_pre = gelu_pull(grad_active)[0].astype(jnp.bfloat16)
    grad_up_bias = jnp.sum(grad_pre.astype(jnp.float32), axis=0)[:, None]
    grad_up = contract(normed_two, grad_pre, 0, 0)
    grad_normed_two = lax.psum(contract(grad_pre, up_full, 1, 1), "tp")
    _, norm_pull_two = jax.vjp(layer_norm, middle, gain_two, shift_two)
    grad_mid_part, grad_gain_two, grad_shift_two = norm_pull_two(grad_normed_two)
    grad_middle = grad_res + grad_mid_part
    grad_att = grad_middle.astype(jnp.bfloat16)
    grad_proj_bias = jnp.sum(grad_att.astype(jnp.float32), axis=0)
    grad_proj = contract(grad_att, context, 0, 0)
    grad_context = (
        jnp.dot(grad_att, proj_full, preferred_element_type=jnp.float32)
        .astype(jnp.bfloat16)
        .reshape(head_shape)
    )
    scores_again = attn_scores(query_heads, key_all, key_valid)
    prob_again = jnp.exp(scores_again - log_total)
    grad_prob = jnp.einsum(
        "bqhd,bkhd->bhqk", grad_context, value_all, preferred_element_type=jnp.float32
    )
    grad_scores = (
        prob_again * (grad_prob - jnp.sum(prob_again * grad_prob, axis=-1, keepdims=True))
    ).astype(jnp.bfloat16)
    score_scale = HD ** (-0.5)
    grad_query = (
        jnp.einsum("bhqk,bkhd->bqhd", grad_scores, key_all, preferred_element_type=jnp.float32)
        * score_scale
    )
    grad_query = grad_query.astype(jnp.bfloat16).reshape(row_count, local_width)
    key_terms = (
        jnp.einsum("bhqk,bqhd->bkhd", grad_scores, query_heads, preferred_element_type=jnp.float32)
        * score_scale
    )
    value_terms = jnp.einsum(
        "bhqk,bqhd->bkhd",
        prob_again.astype(jnp.bfloat16),
        grad_context,
        preferred_element_type=jnp.float32,
    )
    key_summed, value_summed = (
        lax.psum_scatter(key_terms, "ctx", scatter_dimension=1, tiled=True),
        lax.psum_scatter(value_terms, "ctx", scatter_dimension=1, tiled=True),
    )
    grad_key = key_summed.astype(jnp.bfloat16).reshape(row_count, local_width)
    grad_value = value_summed.astype(jnp.bfloat16).reshape(row_count, local_width)
    grad_packed = jnp.stack([grad_query, grad_key, grad_value], axis=1).reshape(
        row_count, 3 * local_width
    )
    grad_qkv = contract(normed, grad_packed, 0, 0).reshape(D, 3, local_width)
    grad_qv_bias = jnp.concatenate(
        [
            jnp.sum(grad_query.astype(jnp.float32), axis=0),
            jnp.sum(grad_value.astype(jnp.float32), axis=0),
        ]
    )[:, None]
    grad_normed = lax.psum(contract(grad_packed, qkv_flat, 1, 1).astype(jnp.bfloat16), "tp").astype(
        jnp.float32
    )
    _, norm_pull_one = jax.vjp(layer_norm, entering, gain_one, shift_one)
    grad_enter_part, grad_gain_one, grad_shift_one = norm_pull_one(grad_normed)
    grad_inputs = ((grad_middle + grad_enter_part) * row_valid).reshape(images, half_slots, D)
    summed = (
        lax.psum_scatter(grad_gain_one, ("fsdp", "ctx"), scatter_dimension=0, tiled=True),
        lax.psum_scatter(grad_shift_one, ("fsdp", "ctx"), scatter_dimension=0, tiled=True),
        lax.psum_scatter(grad_qkv, ("fsdp", "ctx"), scatter_dimension=0, tiled=True),
        lax.psum_scatter(grad_qv_bias, ("fsdp", "ctx"), scatter_dimension=0, tiled=True),
        lax.psum_scatter(grad_proj, ("fsdp", "ctx"), scatter_dimension=0, tiled=True),
        lax.psum_scatter(grad_proj_bias, ("fsdp", "ctx"), scatter_dimension=0, tiled=True),
        lax.psum_scatter(grad_gain_two, ("fsdp", "ctx"), scatter_dimension=0, tiled=True),
        lax.psum_scatter(grad_shift_two, ("fsdp", "ctx"), scatter_dimension=0, tiled=True),
        lax.psum_scatter(grad_up, ("fsdp", "ctx"), scatter_dimension=0, tiled=True),
        lax.psum_scatter(grad_up_bias, ("fsdp", "ctx"), scatter_dimension=0, tiled=True),
        lax.psum_scatter(grad_down, ("fsdp", "ctx"), scatter_dimension=0, tiled=True),
        lax.psum_scatter(grad_down_bias, ("fsdp", "ctx"), scatter_dimension=0, tiled=True),
    )
    return (
        output,
        grad_inputs,
        summed[0],
        summed[1],
        summed[2],
        summed[3],
        summed[4],
        summed[5],
        summed[6],
        summed[7],
        summed[8],
        summed[9],
        summed[10],
        summed[11],
        rms,
    )


def solution(mesh):
    in_specs = (
        P("fsdp", "ctx", None),
        P("fsdp"),
        P("fsdp", "ctx", None),
        P(("fsdp", "ctx")),
        P(("fsdp", "ctx")),
        P(("fsdp", "ctx"), None, "tp"),
        P(("fsdp", "ctx"), "tp"),
        P(("fsdp", "ctx"), "tp"),
        P(("fsdp", "ctx")),
        P(("fsdp", "ctx")),
        P(("fsdp", "ctx")),
        P(("fsdp", "ctx"), "tp"),
        P(("fsdp", "ctx"), "tp"),
        P(("fsdp", "ctx"), "tp"),
        P(("fsdp", "ctx")),
    )
    out_specs = (
        P("fsdp", "ctx", None),
        P("fsdp", "ctx", None),
        P(("fsdp", "ctx")),
        P(("fsdp", "ctx")),
        P(("fsdp", "ctx"), None, "tp"),
        P(("fsdp", "ctx"), "tp"),
        P(("fsdp", "ctx"), "tp"),
        P(("fsdp", "ctx")),
        P(("fsdp", "ctx")),
        P(("fsdp", "ctx")),
        P(("fsdp", "ctx"), "tp"),
        P(("fsdp", "ctx"), "tp"),
        P(("fsdp", "ctx"), "tp"),
        P(("fsdp", "ctx")),
        P(),
    )
    return jax.shard_map(body, mesh=mesh, in_specs=in_specs, out_specs=out_specs, check_vma=False)
```

profile of v0, /device:TPU:0, one launch (start us, length us, event | category | flops | bytes accessed | tf_op | source)
XLA Modules:
  0.0 852.9 jit_solution(4844973030946835387)
XLA Ops:
  8.7 1.3 fusion.71
  16.6 63.5 %all-reduce.14 = (bf16[1024]{0:T(1024)(128)(2,1)S(1)}, bf16[1024]{0:T(1024)(128)(2,1)S(1)}, bf16[1024]{0:T(1024)(128)(2,1)S(1)}, bf16[1024]{0:T(1024)(128)(2,1)S...) all-reduce(bf16[1024]{0:T(1024)(128)(2,1)S(1)} %dynamic-update-slic, ...), channel_id=1, replica_groups=mesh['fsdp'=8,'ctx'=2,'tp'=2] {'fsdp','ctx'}, use_global_device_ids=true, to_apply=%add.2 | all-reduce | flops 7168 | bytes 28672
  81.9 1.2 fusion.25
  83.8 3.2 copy.67
  87.0 1.2 fusion
  89.7 2.3 all_gather.47
  92.6 2.4 all_gather.46
  96.1 1.5 fusion.72
  99.4 2.7 fusion.73
  103.3 17.4 %all_gather.53 = bf16[2048,1]{0,1:T(2,128)(2,1)S(1)} all-gather(bf16[128,1]{0,1:T(2,128)(2,1)S(1)} %copy-done.27), channel_id=1, replica_groups=mesh['fsdp'=8,'ctx'=2,'tp'=2] {'fsdp','ctx'}, dimensions={0}, use_global_device_ids=true | all-gather | bytes 4352 | tf_op jit(solution)/shard_map/all_gather | solution.py:60
  120.8 10.3 %all-reduce.20.cloned.1.call-done = f32[160,1024]{1,0:T(8,128)} async-done(((f32[160,1024]{1,0:T(8,128)}), f32[160,1024]{1,0:T(8,128)}) %all-reduce.20.cloned.1.call-update) | async-done | bytes 655376 | tf_op jit(solution)/shard_map/psum | solution.py:120
  131.0 1.3 fusion.67
  132.6 50.9 %all-gather.9.cloned.1.call-done = bf16[1024,2048]{1,0:T(8,128)(2,1)} async-done(((bf16[64,2048]{1,0:T(8,128)(2,1)}), bf16[1024,2048]{1,0:T(8,128)(2,1)}) %all-gather.9.cloned.1.call-update) | async-done | bytes 4194320 | tf_op jit(solution)/shard_map/all_gather | solution.py:59
  183.5 7.1 multiply_convert_fusion.1
  190.6 43.8 %all-gather.11.cloned.1.call-done = bf16[1024,2048]{1,0:T(8,128)(2,1)} async-done(((bf16[64,2048]{1,0:T(8,128)(2,1)}), bf16[1024,2048]{1,0:T(8,128)(2,1)}) %all-gather.11.cloned.1.call-update) | async-done | bytes 4194320 | tf_op jit(solution)/shard_map/all_gather | solution.py:61
  234.4 4.7 convolution_convert_fusion
  239.1 7.2 convert_reduce_fusion
  247.2 2.4 fusion.74
  249.9 12.2 %all-reduce.22.cloned.1.call-done = bf16[160,1024]{1,0:T(8,128)(2,1)} async-done(((bf16[160,1024]{1,0:T(8,128)(2,1)}), bf16[160,1024]{1,0:T(8,128)(2,1)}) %all-reduce.22.cloned.1.call-update) | async-done | bytes 327696 | tf_op jit(solution)/shard_map/psum | solution.py:128
  262.1 33.8 %all-reduce.24.cloned.1.call-done = f32[160,1024]{1,0:T(8,128)} async-done(((f32[160,1024]{1,0:T(8,128)}), f32[160,1024]{1,0:T(8,128)}) %all-reduce.24.cloned.1.call-update) | async-done | bytes 655376 | tf_op jit(solution)/shard_map/psum | solution.py:151
  296.0 3.4 fusion.36
  303.2 2.4 convolution_bitcast_fusion.1
  305.7 2.6 copy.86
  308.3 2.5 reshape.397
  310.9 1.9 multiply_reduce_fusion
  314.2 1.2 fusion.10
  315.5 1.6 copy.84
  318.4 1.4 copy.90
  322.3 8.1 reduce-scatter.25.cloned.1.call-done
  333.3 3.9 fusion.11
  337.2 1.8 fusion.75
  339.1 3.9 fusion.38
  344.1 4.6 fusion.62
  349.9 4.5 convolution_bitcast_fusion
  354.4 9.1 %copy.92 = f32[1024,2048]{1,0:T(8,128)} copy(f32[1024,2048]{0,1:T(8,128)} %convolution_bitcast_fusion) | data formatting | bytes 16777216
  364.9 27.8 %reduce-scatter.31.cloned.1.call-done = f32[128,1]{1,0:T(8,128)} async-done(((f32[2048,1]{1,0:T(8,128)}), f32[128,1]{1,0:T(8,128)}) %reduce-scatter.31.cloned.1.call-update) | async-done | bytes 528
  392.7 1.4 copy.91
  394.1 57.4 %reduce-scatter.29.cloned.1.call-done = f32[64,1]{1,0:T(8,128)} async-done(((f32[1024,1]{1,0:T(8,128)}), f32[64,1]{1,0:T(8,128)}) %reduce-scatter.29.cloned.1.call-update) | async-done | bytes 272
  451.5 1.3 copy.89
  452.8 24.2 %all-reduce.26.cloned.1.call-done = bf16[160,1024]{1,0:T(8,128)(2,1)} async-done(((bf16[160,1024]{1,0:T(8,128)(2,1)}), bf16[160,1024]{1,0:T(8,128)(2,1)}) %all-reduce.26.cloned.1.call-update) | async-done | bytes 327696 | tf_op jit(solution)/shard_map/psum | solution.py:203
  477.0 2.1 fusion.32
  479.1 3.3 stack.27
  482.5 1.4 fusion.31
  484.0 1.2 convert_reduce_fusion.2
  485.2 61.3 %all-reduce.13 = (f32[1024]{0:T(1024)S(1)}, f32[1024]{0:T(1024)S(1)}, f32[1024]{0:T(1024)S(1)}, f32[1024]{0:T(1024)S(1)}, f32[1024]{0:T(1024)S(1)}, /*index=5*/f32[1024]{0:T(1024)S(1)}, f32[5]{0:T(128)S(1)}, f32[]{:T(128)}) all-reduce(f32[1024]{0:T(1024)S(1)} %get-tuple-element.77, ...), channel_id=4, replica_groups=mesh['fsdp'=8,'ctx'=2,'tp'=2] {'fsdp','ctx'}, use_global_device_ids=true, to_apply=%region_18.19.clone | all-reduce | flops 6150 | bytes 49200
  551.2 80.4 %reduce-scatter.19.cloned.1.call-done = f32[64,3,512]{2,0,1:T(8,128)} async-done(((f32[1024,3,512]{2,0,1:T(8,128)}), f32[64,3,512]{2,0,1:T(8,128)}) %reduce-scatter.19.cloned.1.call-update) | async-done | bytes 393232 | tf_op jit(solution)/shard_map/reduce_scatter | solution.py:212
  631.7 107.0 %reduce-scatter.23.cloned.1.call-done = f32[64,2048]{1,0:T(8,128)} async-done(((f32[1024,2048]{1,0:T(8,128)}), f32[64,2048]{1,0:T(8,128)}) %reduce-scatter.23.cloned.1.call-update) | async-done | bytes 524304 | tf_op jit(solution)/shard_map/reduce_scatter | solution.py:218
  738.7 107.6 %reduce-scatter.33.cloned.1.call-done = f32[64,2048]{1,0:T(8,128)} async-done(((f32[1024,2048]{1,0:T(8,128)}), f32[64,2048]{1,0:T(8,128)}) %reduce-scatter.33.cloned.1.call-update) | async-done | bytes 524304
  (168 shorter events, 35.6 us)
Async XLA Ops:
  7.2 76.6 %all-gather.5.cloned.1.call-start = ((), (), s32[]{:S(2)}) async-start(), calls=%async_computation.8 | async-start | bytes 3342336 | tf_op jit(solution)/shard_map/all_gather | solution.py:53
  7.9 91.4 %all-gather.7.cloned.1.call-start = ((), (), s32[]{:S(2)}) async-start(), calls=%async_computation.9 | async-start | bytes 1114112 | tf_op jit(solution)/shard_map/all_gather | solution.py:55
  8.7 122.4 %all-reduce.20.cloned.1.call-start = ((), (), s32[]{:S(2)}) async-start(), calls=%async_computation.10 | async-start | bytes 1310720 | tf_op jit(solution)/shard_map/psum | solution.py:120
  83.1 0.5 copy-start.22
  83.8 3.2 copy-start
  97.6 1.0 copy-start.17
  99.3 2.7 copy-start.18
  99.4 3.9 copy-start.27
  102.1 81.4 %all-gather.9.cloned.1.call-start = ((), (), s32[]{:S(2)}) async-start(), calls=%async_computation.11 | async-start | bytes 4456448 | tf_op jit(solution)/shard_map/all_gather | solution.py:59
  102.6 131.8 %all-gather.11.cloned.1.call-start = ((), (), s32[]{:S(2)}) async-start(), calls=%async_computation.12 | async-start | bytes 4456448 | tf_op jit(solution)/shard_map/all_gather | solution.py:61
  103.2 158.9 %all-reduce.22.cloned.1.call-start = ((), (), s32[]{:S(2)}) async-start(), calls=%async_computation.13 | async-start | bytes 655360 | tf_op jit(solution)/shard_map/psum | solution.py:128
  239.1 56.9 %all-reduce.24.cloned.1.call-start = ((), (), s32[]{:S(2)}) async-start(), calls=%async_computation.14 | async-start | bytes 1310720 | tf_op jit(solution)/shard_map/psum | solution.py:151
  239.1 8.1 copy-start.5
  246.4 0.8 copy-start.14
  249.6 71.1 %reduce-scatter.27.cloned.1.call-start = ((), (), s32[]{:S(2)}) async-start(), calls=%async_computation.20 | async-start | bytes 983040
  296.0 3.4 copy-start.13
  299.3 1.2 copy-start.11
  299.4 2.7 copy-start.6
  299.7 0.9 copy-start.3
  299.7 1.6 copy-start.24
  301.3 0.7 copy-start.9
  310.8 19.6 %reduce-scatter.25.cloned.1.call-start = ((), (), s32[]{:S(2)}) async-start(), calls=%async_computation.19 | async-start | bytes 983040
  312.8 1.5 copy-start.16
  313.3 1.0 copy-start.1
  317.1 1.3 copy-start.26
  318.3 1.5 copy-start.2
  318.3 74.3 %reduce-scatter.31.cloned.1.call-start = ((), (), s32[]{:S(2)}) async-start(), calls=%async_computation.22 | async-start | bytes 1114112
  319.8 131.7 %reduce-scatter.29.cloned.1.call-start = ((), (), s32[]{:S(2)}) async-start(), calls=%async_computation.21 | async-start | bytes 557056
  333.2 4.0 copy-start.10
  333.2 4.0 copy-start.19
  333.2 143.8 %all-reduce.26.cloned.1.call-start = ((), (), s32[]{:S(2)}) async-start(), calls=%async_computation.15 | async-start | bytes 655360 | tf_op jit(solution)/shard_map/psum | solution.py:203
  337.2 214.1 %reduce-scatter.21.cloned.1.call-start = ((), (), s32[]{:S(2)}) async-start(), calls=%async_computation.17 | async-start | bytes 2228224 | tf_op jit(solution)/shard_map/reduce_scatter | solution.py:214
  339.1 292.6 %reduce-scatter.19.cloned.1.call-start = ((), (), s32[]{:S(2)}) async-start(), calls=%async_computation.16 | async-start | bytes 6684672 | tf_op jit(solution)/shard_map/reduce_scatter | solution.py:212
  343.0 1.1 copy-start.15
  343.0 395.7 %reduce-scatter.23.cloned.1.call-start = ((), (), s32[]{:S(2)}) async-start(), calls=%async_computation.18 | async-start | bytes 8912896 | tf_op jit(solution)/shard_map/reduce_scatter | solution.py:218
  348.7 1.1 copy-start.7
  348.7 1.2 copy-start.12
  348.7 497.6 %reduce-scatter.33.cloned.1.call-start = ((), (), s32[]{:S(2)}) async-start(), calls=%async_computation.23 | async-start | bytes 8912896
  363.5 119.0 %copy-start.23 = (f32[160]{0:T(256)S(1)}, f32[160]{0:T(256)}, u32[]{:S(2)}) copy-start(f32[160]{0:T(256)} %copy-done.22) | copy-start | bytes 1924
  363.5 120.4 %copy-start.4 = (f32[160,1024]{1,0:T(8,128)S(1)}, f32[160,1024]{1,0:T(8,128)}, u32[]{:S(2)}) copy-start(f32[160,1024]{1,0:T(8,128)} %copy-done.3) | copy-start | bytes 1966084
  363.5 120.4 %copy-start.25 = (f32[160]{0:T(256)S(1)}, f32[160]{0:T(256)}, u32[]{:S(2)}) copy-start(f32[160]{0:T(256)} %copy-done.24) | copy-start | bytes 1924
  477.0 6.9 copy-start.8
  483.9 1.3 copy-start.20
  483.9 1.3 copy-start.21
Sparse Core Ops, SparseCore 0:
  10.2 48.3 all-gather.4
  60.7 36.5 all-gather.6
  102.2 28.8 all-reduce.19
  133.1 50.3 all-gather.8
  185.5 48.8 all-gather.10
  239.2 22.8 all-reduce.21
  264.4 31.5 all-reduce.23
  310.9 8.0 reduce-scatter.26
  321.3 9.1 reduce-scatter.24
  333.9 58.6 reduce-scatter.30
  396.2 55.2 reduce-scatter.28
  453.6 23.3 all-reduce.25
  481.4 61.9 reduce-scatter.20
  547.7 83.9 reduce-scatter.18
  636.1 102.5 reduce-scatter.22
  743.2 103.0 reduce-scatter.32
where the time goes:
time: 854 us; the launch traced here: 853 us
  waiting for transfers between devices  566 us (66%)
  blocking collectives  147 us (17%)
  local copies, waits for them, and re-layouts  52.8 us (6%)
  matrix products  52.7 us (6%)
  between operations  17.2 us (2%)
  other arithmetic  15.9 us (2%)
    unnamed x21, waiting for transfers between devices  204 us
    unnamed x2, blocking collectives  125 us
    reduce_scatter x1, waiting for transfers between devices, body(): lax.psum_scatter(grad_up, ('fsdp', 'ctx'), scatter_dimension=0, tiled=True)  107 us
    reduce_scatter x1, waiting for transfers between devices, body(): lax.psum_scatter(grad_qkv, ('fsdp', 'ctx'), scatter_dimension=0, tiled=True)  80.4 us
    all_gather x1, waiting for transfers between devices, body(): lax.all_gather(w_up, ('fsdp', 'ctx'), axis=0, tiled=True)  50.9 us
    all_gather x1, waiting for transfers between devices, body(): lax.all_gather(w_down, ('fsdp', 'ctx'), axis=0, tiled=True)  43.8 us
    unnamed x90, local copies, waits for them, and re-layouts  41.7 us
    psum x1, waiting for transfers between devices, body(): grad_normed_two = lax.psum(contract(grad_pre, up_full, 1, 1), 'tp')  33.8 us
  transfers between devices with their start and end apart: 16, of which 12 were waited for; matrix products, arithmetic and copies ran while one was open for 11% of the time, Pallas kernels for 0%

commit v1 on v0

--- a/solution.py
+++ b/solution.py
@@ -148,7 +148,7 @@
     grad_pre = gelu_pull(grad_active)[0].astype(jnp.bfloat16)
     grad_up_bias = jnp.sum(grad_pre.astype(jnp.float32), axis=0)[:, None]
     grad_up = contract(normed_two, grad_pre, 0, 0)
-    grad_normed_two = lax.psum(contract(grad_pre, up_full, 1, 1), "tp")
+    grad_normed_two = jnp.sum(lax.all_gather(contract(grad_pre, up_full, 1, 1), "tp"), axis=0)
     _, norm_pull_two = jax.vjp(layer_norm, middle, gain_two, shift_two)
     grad_mid_part, grad_gain_two, grad_shift_two = norm_pull_two(grad_normed_two)
     grad_middle = grad_res + grad_mid_part

time: 854 us -> 853 us (level)
    psum x1 -> x0, waiting for transfers between devices: 33.8 us -> none  [body(): grad_normed_two = lax.psum(contract(grad_pre, up_full, 1, 1), 'tp')]
    all_gather x0 -> x1, waiting for transfers between devices: none -> 17.9 us  [body(): lax.all_gather(contract(grad_pre, up_full, 1, 1), 'tp')]
    psum x1, waiting for transfers between devices: 12.2 us -> 24.9 us  [body(): lax.psum(contract(active, down_full, 1, 1).astype(jnp.bfloat16), 'tp')]
    unnamed x90 -> x96, local copies, waits for them, and re-layouts: 41.7 us -> 42.3 us
where the time goes in v1:
time: 853 us; the launch traced here: 852 us
  waiting for transfers between devices  563 us (66%)
  blocking collectives  148 us (17%)
  local copies, waits for them, and re-layouts  52.8 us (6%)
  matrix products  51.7 us (6%)
  other arithmetic  18.2 us (2%)
  between operations  17.2 us (2%)
    unnamed x21, waiting for transfers between devices  203 us
    unnamed x2, blocking collectives  125 us
    reduce_scatter x1, waiting for transfers between devices, body(): lax.psum_scatter(grad_up, ('fsdp', 'ctx'), scatter_dimension=0, tiled=True)  107 us
    reduce_scatter x1, waiting for transfers between devices, body(): lax.psum_scatter(grad_qkv, ('fsdp', 'ctx'), scatter_dimension=0, tiled=True)  80.4 us
    all_gather x1, waiting for transfers between devices, body(): lax.all_gather(w_up, ('fsdp', 'ctx'), axis=0, tiled=True)  50.9 us
    all_gather x1, waiting for transfers between devices, body(): lax.all_gather(w_down, ('fsdp', 'ctx'), axis=0, tiled=True)  43.8 us
    unnamed x96, local copies, waits for them, and re-layouts  42.3 us
    dot_general x8, matrix products, contract(): lax.dot_general(left, right, (((left_dim,), (right_dim,)), ((), ())), pre...  28.3 us
  transfers between devices with their start and end apart: 16, of which 12 were waited for; matrix products, arithmetic and copies ran while one was open for 11% of the time, Pallas kernels for 0%

profile of v1, /device:TPU:0, one launch (start us, length us, event | category | flops | bytes accessed | tf_op | source)
XLA Modules:
  0.0 851.6 jit_solution(8293648787805773083)
XLA Ops:
  10.6 1.2 fusion.25
  11.9 1.3 fusion.71
  19.7 63.4 %all-reduce.14 = (bf16[1024]{0:T(1024)(128)(2,1)S(1)}, bf16[1024]{0:T(1024)(128)(2,1)S(1)}, bf16[1024]{0:T(1024)(128)(2,1)S(1)}, bf16[1024]{0:T(1024)(128)(2,1)S...) all-reduce(bf16[1024]{0:T(1024)(128)(2,1)S(1)} %dynamic-update-slic, ...), channel_id=1, replica_groups=mesh['fsdp'=8,'ctx'=2,'tp'=2] {'fsdp','ctx'}, use_global_device_ids=true, to_apply=%add.2 | all-reduce | flops 7168 | bytes 28672
  83.3 3.2 copy.67
  86.6 1.2 fusion
  89.0 2.4 all_gather.53
  92.1 2.3 all_gather.52
  98.5 2.7 fusion.73
  102.4 18.4 %all_gather.59 = bf16[2048,1]{0,1:T(2,128)(2,1)S(1)} all-gather(bf16[128,1]{0,1:T(2,128)(2,1)S(1)} %copy-done.30), channel_id=1, replica_groups=mesh['fsdp'=8,'ctx'=2,'tp'=2] {'fsdp','ctx'}, dimensions={0}, use_global_device_ids=true | all-gather | bytes 4352 | tf_op jit(solution)/shard_map/all_gather | solution.py:60
  120.8 9.9 %all-reduce.19.cloned.1.call-done = f32[160,1024]{1,0:T(8,128)} async-done(((f32[160,1024]{1,0:T(8,128)}), f32[160,1024]{1,0:T(8,128)}) %all-reduce.19.cloned.1.call-update) | async-done | bytes 655376 | tf_op jit(solution)/shard_map/psum | solution.py:120
  130.7 1.3 fusion.67
  132.3 50.9 %all-gather.11.cloned.1.call-done = bf16[1024,2048]{1,0:T(8,128)(2,1)} async-done(((bf16[64,2048]{1,0:T(8,128)(2,1)}), bf16[1024,2048]{1,0:T(8,128)(2,1)}) %all-gather.11.cloned.1.call-update) | async-done | bytes 4194320 | tf_op jit(solution)/shard_map/all_gather | solution.py:59
  183.2 7.1 multiply_convert_fusion.1
  190.3 43.8 %all-gather.13.cloned.1.call-done = bf16[1024,2048]{1,0:T(8,128)(2,1)} async-done(((bf16[64,2048]{1,0:T(8,128)(2,1)}), bf16[1024,2048]{1,0:T(8,128)(2,1)}) %all-gather.13.cloned.1.call-update) | async-done | bytes 4194320 | tf_op jit(solution)/shard_map/all_gather | solution.py:61
  234.1 7.2 convert_reduce_fusion
  242.2 2.4 fusion.74
  244.6 4.7 convolution_convert_fusion
  249.6 17.9 %all-gather.15.cloned.1.call-done = f32[320,1024]{1,0:T(8,128)} async-done(((f32[160,1024]{1,0:T(8,128)}), f32[320,1024]{1,0:T(8,128)}) %all-gather.15.cloned.1.call-update) | async-done | bytes 1310736 | tf_op jit(solution)/shard_map/all_gather | solution.py:151
  267.5 2.3 reduce_sum.244
  269.8 24.9 %all-reduce.21.cloned.1.call-done = bf16[160,1024]{1,0:T(8,128)(2,1)} async-done(((bf16[160,1024]{1,0:T(8,128)(2,1)}), bf16[160,1024]{1,0:T(8,128)(2,1)}) %all-reduce.21.cloned.1.call-update) | async-done | bytes 327696 | tf_op jit(solution)/shard_map/psum | solution.py:128
  294.7 3.3 fusion.36
  301.9 2.4 convolution_bitcast_fusion.1
  304.3 2.6 copy.86
  307.0 2.5 reshape.398
  309.5 1.9 multiply_reduce_fusion
  312.9 1.2 fusion.10
  314.1 1.6 copy.84
  317.1 1.4 copy.90
  322.2 6.9 reduce-scatter.25.cloned.1.call-done
  330.8 3.8 fusion.11
  334.7 1.8 fusion.75
  336.6 3.9 fusion.38
  341.5 4.6 fusion.62
  347.3 4.5 convolution_bitcast_fusion
  351.9 9.1 %copy.92 = f32[1024,2048]{1,0:T(8,128)} copy(f32[1024,2048]{0,1:T(8,128)} %convolution_bitcast_fusion) | data formatting | bytes 16777216
  362.4 29.0 %reduce-scatter.31.cloned.1.call-done = f32[128,1]{1,0:T(8,128)} async-done(((f32[2048,1]{1,0:T(8,128)}), f32[128,1]{1,0:T(8,128)}) %reduce-scatter.31.cloned.1.call-update) | async-done | bytes 528
  391.3 1.4 copy.91
  392.9 57.3 %reduce-scatter.29.cloned.1.call-done = f32[64,1]{1,0:T(8,128)} async-done(((f32[1024,1]{1,0:T(8,128)}), f32[64,1]{1,0:T(8,128)}) %reduce-scatter.29.cloned.1.call-update) | async-done | bytes 272
  450.1 1.3 copy.89
  451.5 24.2 %all-reduce.23.cloned.1.call-done = bf16[160,1024]{1,0:T(8,128)(2,1)} async-done(((bf16[160,1024]{1,0:T(8,128)(2,1)}), bf16[160,1024]{1,0:T(8,128)(2,1)}) %all-reduce.23.cloned.1.call-update) | async-done | bytes 327696 | tf_op jit(solution)/shard_map/psum | solution.py:203
  475.7 2.1 fusion.32
  477.8 3.3 stack.27
  481.1 1.4 fusion.31
  482.6 1.2 convert_reduce_fusion.2
  483.8 61.3 %all-reduce.13 = (f32[1024]{0:T(1024)S(1)}, f32[1024]{0:T(1024)S(1)}, f32[1024]{0:T(1024)S(1)}, f32[1024]{0:T(1024)S(1)}, f32[1024]{0:T(1024)S(1)}, /*index=5*/f32[1024]{0:T(1024)S(1)}, f32[5]{0:T(128)S(1)}, f32[]{:T(128)}) all-reduce(f32[1024]{0:T(1024)S(1)} %get-tuple-element.77, ...), channel_id=5, replica_groups=mesh['fsdp'=8,'ctx'=2,'tp'=2] {'fsdp','ctx'}, use_global_device_ids=true, to_apply=%region_18.19.clone | all-reduce | flops 6150 | bytes 49200
  549.9 80.4 %reduce-scatter.19.cloned.1.call-done = f32[64,3,512]{2,0,1:T(8,128)} async-done(((f32[1024,3,512]{2,0,1:T(8,128)}), f32[64,3,512]{2,0,1:T(8,128)}) %reduce-scatter.19.cloned.1.call-update) | async-done | bytes 393232 | tf_op jit(solution)/shard_map/reduce_scatter | solution.py:212
  630.3 107.2 %reduce-scatter.23.cloned.1.call-done = f32[64,2048]{1,0:T(8,128)} async-done(((f32[1024,2048]{1,0:T(8,128)}), f32[64,2048]{1,0:T(8,128)}) %reduce-scatter.23.cloned.1.call-update) | async-done | bytes 524304 | tf_op jit(solution)/shard_map/reduce_scatter | solution.py:218
  737.4 107.6 %reduce-scatter.33.cloned.1.call-done = f32[64,2048]{1,0:T(8,128)} async-done(((f32[1024,2048]{1,0:T(8,128)}), f32[64,2048]{1,0:T(8,128)}) %reduce-scatter.33.cloned.1.call-update) | async-done | bytes 524304
  (176 shorter events, 36.2 us)
Async XLA Ops:
  7.2 76.1 %all-gather.7.cloned.1.call-start = ((), (), s32[]{:S(2)}) async-start(), calls=%async_computation.8 | async-start | bytes 3342336 | tf_op jit(solution)/shard_map/all_gather | solution.py:53
  7.9 90.5 %all-gather.9.cloned.1.call-start = ((), (), s32[]{:S(2)}) async-start(), calls=%async_computation.9 | async-start | bytes 1114112 | tf_op jit(solution)/shard_map/all_gather | solution.py:55
  8.7 122.1 %all-reduce.19.cloned.1.call-start = ((), (), s32[]{:S(2)}) async-start(), calls=%async_computation.10 | async-start | bytes 1310720 | tf_op jit(solution)/shard_map/psum | solution.py:120
  11.8 71.4 %copy-start.25 = (f32[160]{0:T(256)}, f32[160]{0:T(256)S(1)}, u32[]{:S(2)}) copy-start(f32[160]{0:T(256)S(1)} %fusion.25) | copy-start | bytes 1924
  83.3 3.2 copy-start
  87.8 1.0 copy-start.10
  88.8 3.1 copy-start.11
  96.0 0.7 copy-start.19
  96.7 1.0 copy-start.21
  98.4 2.7 copy-start.22
  98.5 3.9 copy-start.30
  101.2 82.0 %all-gather.11.cloned.1.call-start = ((), (), s32[]{:S(2)}) async-start(), calls=%async_computation.11 | async-start | bytes 4456448 | tf_op jit(solution)/shard_map/all_gather | solution.py:59
  101.7 132.4 %all-gather.13.cloned.1.call-start = ((), (), s32[]{:S(2)}) async-start(), calls=%async_computation.12 | async-start | bytes 4456448 | tf_op jit(solution)/shard_map/all_gather | solution.py:61
  102.3 165.2 %all-gather.15.cloned.1.call-start = ((), (), s32[]{:S(2)}) async-start(), calls=%async_computation.18 | async-start | bytes 1966080 | tf_op jit(solution)/shard_map/all_gather | solution.py:151
  234.1 8.1 copy-start.7
  241.3 0.8 copy-start.17
  244.6 50.2 %all-reduce.21.cloned.1.call-start = ((), (), s32[]{:S(2)}) async-start(), calls=%async_computation.13 | async-start | bytes 655360 | tf_op jit(solution)/shard_map/psum | solution.py:128
  249.3 70.0 %reduce-scatter.27.cloned.1.call-start = ((), (), s32[]{:S(2)}) async-start(), calls=%async_computation.20 | async-start | bytes 983040
  294.7 3.3 copy-start.3
  298.0 1.2 copy-start.15
  298.0 2.7 copy-start.8
  298.3 0.9 copy-start.4
  298.4 1.6 copy-start.27
  300.0 0.7 copy-start.13
  309.5 19.6 %reduce-scatter.25.cloned.1.call-start = ((), (), s32[]{:S(2)}) async-start(), calls=%async_computation.19 | async-start | bytes 983040
  311.4 1.5 copy-start.20
  311.9 1.0 copy-start.1
  315.8 1.3 copy-start.29
  317.0 1.5 copy-start.2
  317.0 74.3 %reduce-scatter.31.cloned.1.call-start = ((), (), s32[]{:S(2)}) async-start(), calls=%async_computation.22 | async-start | bytes 1114112
  318.4 131.7 %reduce-scatter.29.cloned.1.call-start = ((), (), s32[]{:S(2)}) async-start(), calls=%async_computation.21 | async-start | bytes 557056
  330.7 4.0 copy-start.14
  330.7 4.0 copy-start.23
  330.7 144.9 %all-reduce.23.cloned.1.call-start = ((), (), s32[]{:S(2)}) async-start(), calls=%async_computation.14 | async-start | bytes 655360 | tf_op jit(solution)/shard_map/psum | solution.py:203
  334.6 215.2 %reduce-scatter.21.cloned.1.call-start = ((), (), s32[]{:S(2)}) async-start(), calls=%async_computation.16 | async-start | bytes 2228224 | tf_op jit(solution)/shard_map/reduce_scatter | solution.py:214
  336.5 293.7 %reduce-scatter.19.cloned.1.call-start = ((), (), s32[]{:S(2)}) async-start(), calls=%async_computation.15 | async-start | bytes 6684672 | tf_op jit(solution)/shard_map/reduce_scatter | solution.py:212
  340.4 1.1 copy-start.18
  340.5 397.0 %reduce-scatter.23.cloned.1.call-start = ((), (), s32[]{:S(2)}) async-start(), calls=%async_computation.17 | async-start | bytes 8912896 | tf_op jit(solution)/shard_map/reduce_scatter | solution.py:218
  346.2 1.1 copy-start.9
  346.2 1.2 copy-start.16
  346.2 498.9 %reduce-scatter.33.cloned.1.call-start = ((), (), s32[]{:S(2)}) async-start(), calls=%async_computation.23 | async-start | bytes 8912896
  361.0 31.8 %copy-start.6 = (f32[320,1024]{1,0:T(8,128)S(1)}, f32[320,1024]{1,0:T(8,128)}, u32[]{:S(2)}) copy-start(f32[320,1024]{1,0:T(8,128)} %all-gather.15.cloned.1.call-done) | copy-start | bytes 3932164
  361.0 120.1 %copy-start.26 = (f32[160]{0:T(256)S(1)}, f32[160]{0:T(256)}, u32[]{:S(2)}) copy-start(f32[160]{0:T(256)} %copy-done.25) | copy-start | bytes 1924
  392.8 89.8 %copy-start.5 = (f32[160,1024]{1,0:T(8,128)S(1)}, f32[160,1024]{1,0:T(8,128)}, u32[]{:S(2)}) copy-start(f32[160,1024]{1,0:T(8,128)} %copy-done.4) | copy-start | bytes 1966084
  392.8 89.8 %copy-start.28 = (f32[160]{0:T(256)S(1)}, f32[160]{0:T(256)}, u32[]{:S(2)}) copy-start(f32[160]{0:T(256)} %copy-done.27) | copy-start | bytes 1924
  475.7 6.9 copy-start.12
  482.5 1.3 copy-start.24
Sparse Core Ops, SparseCore 0:
  10.2 48.6 all-gather.6
  61.0 36.2 all-gather.8
  101.3 29.4 all-reduce.18
  132.7 50.3 all-gather.10
  185.2 48.8 all-gather.12
  244.7 22.7 all-gather.14
  270.3 24.3 all-reduce.20
  309.6 8.0 reduce-scatter.26
  319.9 9.1 reduce-scatter.24
  332.6 58.6 reduce-scatter.30
  394.9 55.1 reduce-scatter.28
  452.3 23.3 all-reduce.22
  480.0 61.9 reduce-scatter.20
  546.3 83.9 reduce-scatter.18
  634.7 102.6 reduce-scatter.22
  741.9 103.0 reduce-scatter.32
